TPU v7x, 32 devices: a whole 2x2x4 slice. The times are simulated.
32 devices in a mesh: chan: 4 (over y, x), hid: 8 (over z, core).
Axes of the slice: x: 2, y: 2, z: 4, core: 2. Of those that a mesh axis runs over, the one named last changes fastest.
Arguments:
- pixels: bfloat16 [384, 256, 256], P('chan'), may hold values from -6 to 6
- patch_weight: bfloat16 [384, 256, 6144], P('chan', None, 'hid'), may hold values from -0.375 to 0.375
- channel_embed: bfloat16 [384, 6144], P('chan', 'hid'), may hold values from -3 to 3
- pool_query: bfloat16 [48, 6144], P('chan', 'hid'), may hold values from -2.5 to 2.5
- group_mix: bfloat16 [48, 6144], P('chan', 'hid'), may hold values from -3.2 to 3.2
- assign: int32 [384], P('chan'), may hold values from 0 to 47, as said below
- ln_gain: float32 [6144], P('chan'), may hold values from 0.1 to 1.9
- w_qkv: bfloat16 [6144, 3, 6144], P('chan', None, 'hid'), may hold values from -0.078125 to 0.078125
- w_up: bfloat16 [6144, 24576], P('chan', 'hid'), may hold values from -0.078125 to 0.078125
- b_up: float32 [24576], P('hid'), may hold values from -3 to 3
- w_out: bfloat16 [6144, 6144], P('hid', 'chan'), may hold values from -0.078125 to 0.078125
- w_down: bfloat16 [24576, 6144], P('hid', 'chan'), may hold values from -0.0390625 to 0.0390625
Outputs:
- block_out: bfloat16 [256, 6144], P(None, 'chan')
Inputs may be any that keep to these rules, and one draw needn't show every extreme that they name: Channel c belongs to group assign[c]; every group holds exactly 8 channels, and group k's channels all lie among the 96 consecutive channels beginning at channel (k // 12) * 96.
All inputs are finite; a program needn't handle non-finite values.
Results may differ from a plain program's by a relative error of at most 0.02.
Values may be sent and summed in bfloat16 or wider, within the bound.
A program may use at most 320 MiB of HBM per device.

v0:
```python
import math
import jax
import jax.numpy as jnp
from jax import lax
from jax.sharding import PartitionSpec as P

HS = 128
PATCHES = 256
D = 6144
epsilon = 1e-06


def head_norm(values):
    return values * lax.rsqrt(jnp.mean(values * values, axis=-1, keepdims=True) + epsilon)


def finish_rows(qkv_rows, up_rows, b_up, heads_dev):
    rows = qkv_rows.shape[0]
    width = heads_dev * HS
    query_part = (
        head_norm(qkv_rows[:, 0].reshape(rows, heads_dev, HS))
        .astype(jnp.bfloat16)
        .reshape(rows, width)
    )
    key_part = (
        head_norm(qkv_rows[:, 1].reshape(rows, heads_dev, HS))
        .astype(jnp.bfloat16)
        .reshape(rows, width)
    )
    value_part = qkv_rows[:, 2].astype(jnp.bfloat16)
    hidden_part = jax.nn.gelu(up_rows + b_up, approximate=False).astype(jnp.bfloat16)
    return (query_part, key_part, value_part, hidden_part)


def on_device(
    pixels,
    patch_weight,
    channel_embed,
    pool_query,
    group_mix,
    assign,
    ln_gain,
    w_qkv,
    w_up,
    b_up,
    w_out,
    w_down,
):
    chan_count = pixels.shape[0]
    tok_count = pixels.shape[1]
    width_hid = patch_weight.shape[2]
    width_chan = ln_gain.shape[0]
    heads_dev = width_hid // HS
    groups_dev = pool_query.shape[0]
    embedded = jnp.einsum("ctp,cpd->ctd", pixels, patch_weight, preferred_element_type=jnp.float32)
    embedded = embedded + channel_embed.astype(jnp.float32)[:, None, :]
    features = jax.nn.gelu(embedded, approximate=False)
    split = features.reshape(chan_count, tok_count, heads_dev, HS)
    normed = head_norm(split)
    local_group = assign - lax.axis_index("chan") * groups_dev
    member = (local_group[None, :] == jnp.arange(groups_dev, dtype=jnp.int32)[:, None]).astype(
        jnp.float32
    )
    query = jnp.dot(member.T, pool_query.astype(jnp.float32), precision=lax.Precision.HIGHEST)
    query = query.reshape(chan_count, heads_dev, HS)
    score = jnp.einsum("cthe,che->cth", normed, query, precision=lax.Precision.HIGHEST) / math.sqrt(
        HS
    )
    shift = jnp.sqrt(jnp.sum(query * query, axis=-1))
    weight = jnp.exp(score - shift[:, None, :])
    numer = jnp.einsum(
        "kc,cthe->kthe", member, weight[..., None] * split, precision=lax.Precision.HIGHEST
    )
    denom = jnp.einsum("kc,cth->kth", member, weight, precision=lax.Precision.HIGHEST)
    pooled = (numer / denom[..., None]).reshape(groups_dev, tok_count, width_hid)
    partial_value = jnp.einsum(
        "kd,ktd->td", group_mix.astype(jnp.float32), pooled, precision=lax.Precision.HIGHEST
    )
    layer_sum = lax.psum(partial_value.astype(jnp.bfloat16), "chan")
    gathered = lax.all_gather(layer_sum, "hid", axis=1, tiled=True)
    wide = gathered.astype(jnp.float32)
    row_total = jnp.sum(wide, axis=1)
    row_square = jnp.sum(wide * wide, axis=1)
    mine = lax.dynamic_slice_in_dim(gathered, lax.axis_index("chan") * width_chan, width_chan, 1)
    row_mean = row_total / D
    row_var = row_square / D - row_mean * row_mean
    own_cols = mine.astype(jnp.float32)
    normed_input = (
        (own_cols - row_mean[:, None]) * lax.rsqrt(row_var + epsilon)[:, None] * ln_gain
    ).astype(jnp.bfloat16)
    qkv_part = jnp.einsum("td,dke->tke", normed_input, w_qkv, preferred_element_type=jnp.float32)
    up_part = jnp.dot(normed_input, w_up, preferred_element_type=jnp.float32)
    qkv_share, up_share = (
        lax.psum_scatter(
            qkv_part.astype(jnp.bfloat16), "chan", scatter_dimension=0, tiled=True
        ).astype(jnp.float32),
        lax.psum_scatter(
            up_part.astype(jnp.bfloat16), "chan", scatter_dimension=0, tiled=True
        ).astype(jnp.float32),
    )
    query_share, key_share, value_share, hidden_share = finish_rows(
        qkv_share, up_share, b_up, heads_dev
    )
    query_rows, key_rows, value_rows, hidden = (
        lax.all_gather(query_share, "chan", axis=0, tiled=True),
        lax.all_gather(key_share, "chan", axis=0, tiled=True),
        lax.all_gather(value_share, "chan", axis=0, tiled=True),
        lax.all_gather(hidden_share, "chan", axis=0, tiled=True),
    )
    images = tok_count // PATCHES
    queries = query_rows.reshape(images, PATCHES, heads_dev, HS)
    keys = key_rows.reshape(images, PATCHES, heads_dev, HS)
    values = value_rows.reshape(images, PATCHES, heads_dev, HS)
    scores = jnp.einsum("bqhe,bkhe->bhqk", queries, keys, preferred_element_type=jnp.float32) * (
        2.0 / math.sqrt(HS)
    )
    expo = jnp.exp(scores)
    probs = (expo / jnp.sum(expo, axis=-1, keepdims=True)).astype(jnp.bfloat16)
    attended = jnp.einsum("bhqk,bkhe->bqhe", probs, values, preferred_element_type=jnp.float32)
    attended = attended.astype(jnp.bfloat16).reshape(tok_count, width_hid)
    term = jnp.dot(attended, w_out, preferred_element_type=jnp.float32) + jnp.dot(
        hidden, w_down, preferred_element_type=jnp.float32
    )
    mixed = lax.psum(term, "hid")
    return (own_cols + mixed).astype(jnp.bfloat16)


def solution(mesh):
    in_specs = (
        P("chan", None, None),
        P("chan", None, "hid"),
        P("chan", "hid"),
        P("chan", "hid"),
        P("chan", "hid"),
        P("chan"),
        P("chan"),
        P("chan", None, "hid"),
        P("chan", "hid"),
        P("hid"),
        P("hid", "chan"),
        P("hid", "chan"),
    )
    out_specs = P(None, "chan")
    return jax.shard_map(
        on_device, mesh=mesh, in_specs=in_specs, out_specs=out_specs, check_vma=False
    )
```

profile of v0, /device:TPU:0, one launch (start us, length us, event | category | flops | bytes accessed | tf_op | source)
XLA Modules:
  0.0 780.2 jit_solution(2045412981143405703)
XLA Ops:
  11.8 171.0 %fusion.1 = f32[96,256,768]{2,1,0:T(8,128)} fusion(f32[96,768]{1,0:T(8,128)S(1)} %convert_element_type.64, bf16[96,256,256]{2,1,0:T(8,128)(2,1)} %param.12, bf16[96,256,768]{2,1,0:T(8,128)(2,1)} %param.13), kind=kOutput, calls=%fused_computation.2 | convolution fusion | flops 10890510336 | bytes 126124032 | tf_op jit(solution)/shard_map/ctp,cpd->ctd/dot_general | solution.py:55
  182.8 72.9 %copy.57 = f32[96,256,768]{1,2,0:T(8,128)} copy(f32[96,256,768]{2,1,0:T(8,128)} %fusion.1) | data formatting | bytes 150994944 | tf_op jit(solution)/shard_map/mul | solution.py:57
  255.7 23.3 %multiply_reduce_fusion = f32[96,256,6]{1,2,0:T(8,128)S(1)} fusion(f32[96,256,6,128]{1,3,2,0:T(8,128)} %bitcast.4), kind=kLoop, calls=%fused_computation.5 | loop fusion | flops 37601280 | bytes 76087296 | tf_op jit(solution)/shard_map/reduce_sum | solution.py:14
  279.1 43.4 %fusion.2 = f32[96,6,1,256]{3,2,1,0:T(1,128)S(1)} fusion(f32[96,6,128,1]{2,3,1,0:T(1,128)S(1)} %copy-done.1, f32[96,256,6,128]{1,3,2,0:T(8,128)} %bitcast.4, f32[96,256,6]{1,2,0:T(8,128)S(1)} %add_rsqrt_fusion), kind=kOutput, calls=%fused_computation.3 | convolution fusion | flops 245366784 | bytes 76972032 | tf_op jit(solution)/shard_map/cthe,che->cth/dot_general | solution.py:66
  323.4 48.9 %broadcast_multiply_fusion = f32[96,256,6,128]{1,3,2,0:T(8,128)} fusion(f32[96,256,6,128]{1,3,2,0:T(8,128)} %bitcast.4, f32[96,256,6]{1,2,0:T(8,128)S(1)} %copy.59), kind=kLoop, calls=%fused_computation.21 | loop fusion | flops 18874368 | bytes 151584768 | tf_op jit(solution)/shard_map/mul | solution.py:72
  372.3 74.2 %copy.60 = f32[96,256,6,128]{3,0,2,1:T(8,128)} copy(f32[96,256,6,128]{1,3,2,0:T(8,128)} %broadcast_multiply_fusion) | data formatting | bytes 150994944 | tf_op jit(solution)/shard_map/mul | solution.py:72
  446.9 34.5 %broadcast_divide_fusion = f32[12,256,6,128]{3,0,2,1:T(8,128)} fusion(f32[12,256,6]{0,2,1:T(8,128)S(1)} %copy.61, f32[96,256,6,128]{3,0,2,1:T(8,128)} %copy.60, s32[96]{0:T(128)} %copy-done.5), kind=kOutput, calls=%fused_computation.28 | convolution fusion | flops 2720269312 | bytes 85008768 | tf_op jit(solution)/shard_map/kc,cthe->kthe/dot_general | solution.py:71
  481.4 12.1 %copy.86 = f32[12,256,6,128]{1,3,2,0:T(8,128)} copy(f32[12,256,6,128]{3,0,2,1:T(8,128)} %broadcast_divide_fusion) | data formatting | bytes 18874368
  493.5 5.0 fusion.12
  499.5 47.0 %all-reduce.3.cloned.1.call-done = bf16[256,768]{1,0:T(8,128)(2,1)} async-done(((bf16[256,768]{1,0:T(8,128)(2,1)}), bf16[256,768]{1,0:T(8,128)(2,1)}) %all-reduce.3.cloned.1.call-update) | async-done | bytes 393232 | tf_op jit(solution)/shard_map/psum | solution.py:79
  546.5 39.8 %all-gather.4.cloned.1.call-done = bf16[256,6144]{1,0:T(8,128)(2,1)} async-done(((bf16[256,768]{1,0:T(8,128)(2,1)}), bf16[256,6144]{1,0:T(8,128)(2,1)}) %all-gather.4.cloned.1.call-update) | async-done | bytes 3145744 | tf_op jit(solution)/shard_map/all_gather | solution.py:80
  586.3 3.2 convert_reduce_fusion
  589.5 7.8 %convolution_convert_fusion = bf16[256,3072]{1,0:T(8,128)(2,1)} fusion(bf16[1536,3072]{1,0:T(8,128)(2,1)} %param.20, f32[1536]{0:T(1024)S(1)} %copy-done.7, f32[256]{0:T(256)S(1)} %get-tuple-element.12, f32[256]{0:T(256)S(1)} %get-tuple-element.11, bf16[256,6144]{1,0:T(8,128)(2,1)} %all-gather.4.cloned.1.call-done, s32[]{:T(128)S(6)} %select_n.3), kind=kOutput, calls=%fused_computation.29 | convolution fusion | flops 2418671616 | bytes 11804676 | tf_op jit(solution)/shard_map/dot_general | solution.py:92
  597.4 6.5 convolution_convert_fusion.1
  604.2 23.3 %reduce-scatter.5.cloned.1.call-done = bf16[64,3072]{1,0:T(8,128)(2,1)} async-done(((bf16[256,3072]{1,0:T(8,128)(2,1)}), bf16[64,3072]{1,0:T(8,128)(2,1)}) %reduce-scatter.5.cloned.1.call-update) | async-done | bytes 393232 | tf_op jit(solution)/shard_map/reduce_scatter | solution.py:97
  627.6 3.5 fusion.20
  631.1 28.0 %reduce-scatter.3.cloned.1.call-done = bf16[64,3,768]{2,0,1:T(8,128)(2,1)} async-done(((bf16[256,3,768]{2,0,1:T(8,128)(2,1)}), bf16[64,3,768]{2,0,1:T(8,128)(2,1)}) %reduce-scatter.3.cloned.1.call-update) | async-done | bytes 294928 | tf_op jit(solution)/shard_map/reduce_scatter | solution.py:94
  660.0 9.5 %all-gather = bf16[256,1,768]{2,0,1:T(8,128)(2,1)S(1)} all-gather(bf16[64,1,768]{2,0,1:T(8,128)(2,1)S(1)} %slice.13), channel_id=2, replica_groups=mesh['chan'=4,'hid'=8] {'chan'}, dimensions={0}, use_global_device_ids=true | all-gather | bytes 491520 | tf_op jit(solution)/shard_map/all_gather | solution.py:107
  674.9 10.6 %all_gather.18 = bf16[256,768]{1,0:T(8,128)(2,1)S(1)} all-gather(bf16[64,768]{1,0:T(8,128)(2,1)S(1)} %get-tuple-element.7), channel_id=1, replica_groups=mesh['chan'=4,'hid'=8] {'chan'}, dimensions={0}, use_global_device_ids=true | all-gather | bytes 491520 | tf_op jit(solution)/shard_map/all_gather | solution.py:106
  685.6 11.0 %all_gather.17 = bf16[256,768]{1,0:T(8,128)(2,1)S(1)} all-gather(bf16[64,768]{1,0:T(8,128)(2,1)} %get-tuple-element.8), channel_id=1, replica_groups=mesh['chan'=4,'hid'=8] {'chan'}, dimensions={0}, use_global_device_ids=true | all-gather | bytes 491520 | tf_op jit(solution)/shard_map/all_gather | solution.py:105
  698.4 2.4 convolution_convert_fusion.2
  700.8 5.7 fusion.50
  708.5 62.2 %all-reduce.5.cloned.1.call-done = f32[256,1536]{1,0:T(8,128)} async-done(((f32[256,1536]{1,0:T(8,128)}), f32[256,1536]{1,0:T(8,128)}) %all-reduce.5.cloned.1.call-update) | async-done | bytes 1572880 | tf_op jit(solution)/shard_map/psum | solution.py:124
  770.6 2.7 fusion.17
  (66 shorter events, 18.2 us)
Async XLA Ops:
  6.5 699.9 %copy-start = (bf16[768,1536]{1,0:T(8,128)(2,1)S(1)}, bf16[768,1536]{1,0:T(8,128)(2,1)}, u32[]{:S(2)}) copy-start(bf16[768,1536]{1,0:T(8,128)(2,1)} %param.22) | copy-start | bytes 7077892
  6.5 539.9 %all-reduce.3.cloned.1.call-start = ((), (), s32[]{:S(2)}) async-start(), calls=%async_computation.2 | async-start | bytes 786432 | tf_op jit(solution)/shard_map/psum | solution.py:79
  7.3 0.6 copy-start.5
  255.7 23.4 %copy-start.1 = (f32[96,6,128,1]{2,3,1,0:T(1,128)S(1)}, f32[96,6,128,1]{2,3,1,0:T(1,128)}, u32[]{:S(2)}) copy-start(f32[96,6,128,1]{2,3,1,0:T(1,128)} %reshape.112) | copy-start | bytes 884740
  255.7 66.8 %copy-start.3 = (f32[96,6]{0,1:T(8,128)S(1)}, f32[96,6]{0,1:T(8,128)}, u32[]{:S(2)}) copy-start(f32[96,6]{0,1:T(8,128)} %sqrt.7) | copy-start | bytes 6916
  255.7 67.0 %copy-start.6 = (s32[96]{0:T(128)S(1)}, s32[96]{0:T(128)}, u32[]{:S(2)}) copy-start(s32[96]{0:T(128)} %copy-done.5) | copy-start | bytes 1156
  279.0 44.4 %copy-start.2 = (bf16[12,768]{1,0:T(8,128)(2,1)S(1)}, bf16[12,768]{1,0:T(8,128)(2,1)}, u32[]{:S(2)}) copy-start(bf16[12,768]{1,0:T(8,128)(2,1)} %param.16) | copy-start | bytes 55300
  446.9 142.7 %copy-start.7 = (f32[1536]{0:T(1024)S(1)}, f32[1536]{0:T(1024)}, u32[]{:S(2)}) copy-start(f32[1536]{0:T(1024)} %param.18) | copy-start | bytes 18436
  446.9 180.7 %copy-start.4 = (f32[3072]{0:T(1024)S(1)}, f32[3072]{0:T(1024)}, u32[]{:S(2)}) copy-start(f32[3072]{0:T(1024)} %param.21) | copy-start | bytes 36868
  499.5 86.9 %all-gather.4.cloned.1.call-start = ((), (), s32[]{:S(2)}) async-start(), calls=%async_computation.3 | async-start | bytes 3538944 | tf_op jit(solution)/shard_map/all_gather | solution.py:80
  546.5 81.1 %reduce-scatter.5.cloned.1.call-start = ((), (), s32[]{:S(2)}) async-start(), calls=%async_computation.5 | async-start | bytes 1966080 | tf_op jit(solution)/shard_map/reduce_scatter | solution.py:97
  597.4 61.7 %reduce-scatter.3.cloned.1.call-start = ((), (), s32[]{:S(2)}) async-start(), calls=%async_computation.4 | async-start | bytes 1474560 | tf_op jit(solution)/shard_map/reduce_scatter | solution.py:94
  603.9 96.9 %all-gather.6.cloned.1.call-start = ((), (), s32[]{:S(2)}) async-start(), calls=%async_computation.6 | async-start | bytes 1966080 | tf_op jit(solution)/shard_map/all_gather | solution.py:108
  631.1 139.6 %all-reduce.5.cloned.1.call-start = ((), (), s32[]{:S(2)}) async-start(), calls=%async_computation.7 | async-start | bytes 3145728 | tf_op jit(solution)/shard_map/psum | solution.py:124
Sparse Core Ops, SparseCore 0:
  499.6 46.8 all-reduce.2
  548.1 38.1 all-gather.3
  597.5 30.0 reduce-scatter.4
  630.3 28.7 reduce-scatter.2
  660.8 33.7 all-gather.5
  708.6 61.9 all-reduce.4
where the time goes:
time: 783 us; the launch traced here: 780 us
  matrix products  276 us (35%)
  waiting for transfers between devices  200 us (26%)
  local copies, waits for them, and re-layouts  167 us (21%)
  other arithmetic  91.4 us (12%)
  blocking collectives  31.1 us (4%)
  between operations  13.7 us (2%)
    dot_general x1, matrix products, on_device(): jnp.einsum('ctp,cpd->ctd', pixels, patch_weight, preferred_element_type=j...  171 us
    mul x1, local copies, waits for them, and re-layouts, on_device(): weight[..., None] * split  74.2 us
    mul x1, local copies, waits for them, and re-layouts, on_device(): features = jax.nn.gelu(embedded, approximate=False)  72.9 us
    psum x1, waiting for transfers between devices, on_device(): mixed = lax.psum(term, 'hid')  62.2 us
    mul x1, other arithmetic, on_device(): weight[..., None] * split  48.9 us
    psum x1, waiting for transfers between devices, on_device(): layer_sum = lax.psum(partial_value.astype(jnp.bfloat16), 'chan')  47 us
    dot_general x1, matrix products, on_device(): jnp.einsum('cthe,che->cth', normed, query, precision=lax.Precision.HIGHEST)  43.4 us
    all_gather x1, waiting for transfers between devices, on_device(): gathered = lax.all_gather(layer_sum, 'hid', axis=1, tiled=True)  39.8 us
  transfers between devices with their start and end apart: 6, of which 5 were waited for; matrix products, arithmetic and copies ran while one was open for 3% of the time, Pallas kernels for 0%

commit v1 on v0

--- a/solution.py
+++ b/solution.py
@@ -121,7 +121,9 @@
     term = jnp.dot(attended, w_out, preferred_element_type=jnp.float32) + jnp.dot(
         hidden, w_down, preferred_element_type=jnp.float32
     )
-    mixed = lax.psum(term, "hid")
+    mixed = term
+    for hop in (1, 2, 4):
+        mixed = mixed + lax.ppermute(mixed, "hid", [(dev, dev ^ hop) for dev in range(8)])
     return (own_cols + mixed).astype(jnp.bfloat16)
 
 

time: 783 us -> 830 us (1.060)
  waiting for transfers between devices: 200 us -> 244 us
    ppermute x0 -> x3, waiting for transfers between devices: none -> 106 us  [on_device(): lax.ppermute(mixed, 'hid', [(dev, dev ^ hop) for dev in range(8)])]
    psum x1 -> x0, waiting for transfers between devices: 62.2 us -> none  [on_device(): mixed = lax.psum(term, 'hid')]
  transfers between devices with their start and end apart: 6 -> 8, of which waited for: 5 -> 7; matrix products, arithmetic and copies ran while one was open for 3% -> 2% of each run, Pallas kernels for 0% -> 0%
where the time goes in v1:
time: 830 us; the launch traced here: 827 us
  matrix products  275 us (33%)
  waiting for transfers between devices  244 us (29%)
  local copies, waits for them, and re-layouts  167 us (20%)
  other arithmetic  91.6 us (11%)
  blocking collectives  31.1 us (4%)
  between operations  13.4 us (2%)
    dot_general x1, matrix products, on_device(): jnp.einsum('ctp,cpd->ctd', pixels, patch_weight, preferred_element_type=j...  171 us
    ppermute x3, waiting for transfers between devices, on_device(): lax.ppermute(mixed, 'hid', [(dev, dev ^ hop) for dev in range(8)])  106 us
    mul x1, local copies, waits for them, and re-layouts, on_device(): weight[..., None] * split  74.2 us
    mul x1, local copies, waits for them, and re-layouts, on_device(): features = jax.nn.gelu(embedded, approximate=False)  72.9 us
    mul x1, other arithmetic, on_device(): weight[..., None] * split  48.9 us
    psum x1, waiting for transfers between devices, on_device(): layer_sum = lax.psum(partial_value.astype(jnp.bfloat16), 'chan')  47 us
    dot_general x1, matrix products, on_device(): jnp.einsum('cthe,che->cth', normed, query, precision=lax.Precision.HIGHEST)  43.4 us
    all_gather x1, waiting for transfers between devices, on_device(): gathered = lax.all_gather(layer_sum, 'hid', axis=1, tiled=True)  39.8 us
  transfers between devices with their start and end apart: 8, of which 7 were waited for; matrix products, arithmetic and copies ran while one was open for 2% of the time, Pallas kernels for 0%

profile of v1, /device:TPU:0, one launch (start us, length us, event | category | flops | bytes accessed | tf_op | source)
XLA Modules:
  0.0 826.9 jit_solution(12313565523575678462)
XLA Ops:
  11.8 171.0 %fusion.1 = f32[96,256,768]{2,1,0:T(8,128)} fusion(f32[96,768]{1,0:T(8,128)S(1)} %convert_element_type.64, bf16[96,256,256]{2,1,0:T(8,128)(2,1)} %param.12, bf16[96,256,768]{2,1,0:T(8,128)(2,1)} %param.13), kind=kOutput, calls=%fused_computation.2 | convolution fusion | flops 10890510336 | bytes 126124032 | tf_op jit(solution)/shard_map/ctp,cpd->ctd/dot_general | solution.py:55
  182.8 72.9 %copy.57 = f32[96,256,768]{1,2,0:T(8,128)} copy(f32[96,256,768]{2,1,0:T(8,128)} %fusion.1) | data formatting | bytes 150994944 | tf_op jit(solution)/shard_map/mul | solution.py:57
  255.7 23.3 %multiply_reduce_fusion = f32[96,256,6]{1,2,0:T(8,128)S(1)} fusion(f32[96,256,6,128]{1,3,2,0:T(8,128)} %bitcast.4), kind=kLoop, calls=%fused_computation.5 | loop fusion | flops 37601280 | bytes 76087296 | tf_op jit(solution)/shard_map/reduce_sum | solution.py:14
  279.1 43.4 %fusion.2 = f32[96,6,1,256]{3,2,1,0:T(1,128)S(1)} fusion(f32[96,6,128,1]{2,3,1,0:T(1,128)S(1)} %copy-done.1, f32[96,256,6,128]{1,3,2,0:T(8,128)} %bitcast.4, f32[96,256,6]{1,2,0:T(8,128)S(1)} %add_rsqrt_fusion), kind=kOutput, calls=%fused_computation.3 | convolution fusion | flops 245366784 | bytes 76972032 | tf_op jit(solution)/shard_map/cthe,che->cth/dot_general | solution.py:66
  323.4 48.9 %broadcast_multiply_fusion = f32[96,256,6,128]{1,3,2,0:T(8,128)} fusion(f32[96,256,6,128]{1,3,2,0:T(8,128)} %bitcast.4, f32[96,256,6]{1,2,0:T(8,128)S(1)} %copy.59), kind=kLoop, calls=%fused_computation.21 | loop fusion | flops 18874368 | bytes 151584768 | tf_op jit(solution)/shard_map/mul | solution.py:72
  372.3 74.2 %copy.60 = f32[96,256,6,128]{3,0,2,1:T(8,128)} copy(f32[96,256,6,128]{1,3,2,0:T(8,128)} %broadcast_multiply_fusion) | data formatting | bytes 150994944 | tf_op jit(solution)/shard_map/mul | solution.py:72
  446.9 34.5 %broadcast_divide_fusion = f32[12,256,6,128]{3,0,2,1:T(8,128)} fusion(f32[12,256,6]{0,2,1:T(8,128)S(1)} %copy.61, f32[96,256,6,128]{3,0,2,1:T(8,128)} %copy.60, s32[96]{0:T(128)} %copy-done.5), kind=kOutput, calls=%fused_computation.28 | convolution fusion | flops 2720269312 | bytes 85008768 | tf_op jit(solution)/shard_map/kc,cthe->kthe/dot_general | solution.py:71
  481.4 12.1 %copy.86 = f32[12,256,6,128]{1,3,2,0:T(8,128)} copy(f32[12,256,6,128]{3,0,2,1:T(8,128)} %broadcast_divide_fusion) | data formatting | bytes 18874368
  493.5 5.0 fusion.12
  499.5 47.0 %all-reduce.2.cloned.1.call-done = bf16[256,768]{1,0:T(8,128)(2,1)} async-done(((bf16[256,768]{1,0:T(8,128)(2,1)}), bf16[256,768]{1,0:T(8,128)(2,1)}) %all-reduce.2.cloned.1.call-update) | async-done | bytes 393232 | tf_op jit(solution)/shard_map/psum | solution.py:79
  546.5 39.8 %all-gather.4.cloned.1.call-done = bf16[256,6144]{1,0:T(8,128)(2,1)} async-done(((bf16[256,768]{1,0:T(8,128)(2,1)}), bf16[256,6144]{1,0:T(8,128)(2,1)}) %all-gather.4.cloned.1.call-update) | async-done | bytes 3145744 | tf_op jit(solution)/shard_map/all_gather | solution.py:80
  586.3 3.2 convert_reduce_fusion
  589.5 7.8 convolution_convert_fusion
  597.4 6.5 convolution_convert_fusion.1
  604.2 23.3 %reduce-scatter.5.cloned.1.call-done = bf16[64,3072]{1,0:T(8,128)(2,1)} async-done(((bf16[256,3072]{1,0:T(8,128)(2,1)}), bf16[64,3072]{1,0:T(8,128)(2,1)}) %reduce-scatter.5.cloned.1.call-update) | async-done | bytes 393232 | tf_op jit(solution)/shard_map/reduce_scatter | solution.py:97
  627.6 3.5 fusion.20
  631.1 28.0 %reduce-scatter.3.cloned.1.call-done = bf16[64,3,768]{2,0,1:T(8,128)(2,1)} async-done(((bf16[256,3,768]{2,0,1:T(8,128)(2,1)}), bf16[64,3,768]{2,0,1:T(8,128)(2,1)}) %reduce-scatter.3.cloned.1.call-update) | async-done | bytes 294928 | tf_op jit(solution)/shard_map/reduce_scatter | solution.py:94
  660.0 9.5 %all-gather = bf16[256,1,768]{2,0,1:T(8,128)(2,1)S(1)} all-gather(bf16[64,1,768]{2,0,1:T(8,128)(2,1)S(1)} %slice.13), channel_id=2, replica_groups=mesh['chan'=4,'hid'=8] {'chan'}, dimensions={0}, use_global_device_ids=true | all-gather | bytes 491520 | tf_op jit(solution)/shard_map/all_gather | solution.py:107
  674.9 10.6 %all_gather.18 = bf16[256,768]{1,0:T(8,128)(2,1)S(1)} all-gather(bf16[64,768]{1,0:T(8,128)(2,1)S(1)} %get-tuple-element.7), channel_id=1, replica_groups=mesh['chan'=4,'hid'=8] {'chan'}, dimensions={0}, use_global_device_ids=true | all-gather | bytes 491520 | tf_op jit(solution)/shard_map/all_gather | solution.py:106
  685.6 11.0 %all_gather.17 = bf16[256,768]{1,0:T(8,128)(2,1)S(1)} all-gather(bf16[64,768]{1,0:T(8,128)(2,1)} %get-tuple-element.8), channel_id=1, replica_groups=mesh['chan'=4,'hid'=8] {'chan'}, dimensions={0}, use_global_device_ids=true | all-gather | bytes 491520 | tf_op jit(solution)/shard_map/all_gather | solution.py:105
  700.8 5.7 fusion.50
  707.4 3.4 collective-permute-done
  712.6 34.9 %collective-permute-done.1 = f32[256,1536]{1,0:T(8,128)S(1)} collective-permute-done((f32[256,1536]{1,0:T(8,128)S(1)}, f32[256,1536]{1,0:T(8,128)S(1)}, u32[]{:S(2)}, u32[]{:S(2)}) %collective-permute-start.1) | collective-permute-done | bytes 1572896 | tf_op jit(solution)/shard_map/ppermute | solution.py:126
  750.3 67.7 %collective-permute-done.2 = f32[256,1536]{1,0:T(8,128)S(1)} collective-permute-done((f32[256,1536]{1,0:T(8,128)S(1)}, f32[256,1536]{1,0:T(8,128)S(1)}, u32[]{:S(2)}, u32[]{:S(2)}) %collective-permute-start.2) | collective-permute-done | bytes 1572896 | tf_op jit(solution)/shard_map/ppermute | solution.py:126
  (71 shorter events, 26.5 us)
Async XLA Ops:
  6.5 699.9 %copy-start = (bf16[768,1536]{1,0:T(8,128)(2,1)S(1)}, bf16[768,1536]{1,0:T(8,128)(2,1)}, u32[]{:S(2)}) copy-start(bf16[768,1536]{1,0:T(8,128)(2,1)} %param.22) | copy-start | bytes 7077892
  6.5 539.9 %all-reduce.2.cloned.1.call-start = ((), (), s32[]{:S(2)}) async-start(), calls=%async_computation.2 | async-start | bytes 786432 | tf_op jit(solution)/shard_map/psum | solution.py:79
  7.3 0.6 copy-start.5
  255.7 23.4 %copy-start.1 = (f32[96,6,128,1]{2,3,1,0:T(1,128)S(1)}, f32[96,6,128,1]{2,3,1,0:T(1,128)}, u32[]{:S(2)}) copy-start(f32[96,6,128,1]{2,3,1,0:T(1,128)} %reshape.112) | copy-start | bytes 884740
  255.7 66.8 %copy-start.3 = (f32[96,6]{0,1:T(8,128)S(1)}, f32[96,6]{0,1:T(8,128)}, u32[]{:S(2)}) copy-start(f32[96,6]{0,1:T(8,128)} %sqrt.7) | copy-start | bytes 6916
  255.7 67.0 %copy-start.6 = (s32[96]{0:T(128)S(1)}, s32[96]{0:T(128)}, u32[]{:S(2)}) copy-start(s32[96]{0:T(128)} %copy-done.5) | copy-start | bytes 1156
  279.0 44.4 %copy-start.2 = (bf16[12,768]{1,0:T(8,128)(2,1)S(1)}, bf16[12,768]{1,0:T(8,128)(2,1)}, u32[]{:S(2)}) copy-start(bf16[12,768]{1,0:T(8,128)(2,1)} %param.16) | copy-start | bytes 55300
  446.9 142.7 %copy-start.7 = (f32[1536]{0:T(1024)S(1)}, f32[1536]{0:T(1024)}, u32[]{:S(2)}) copy-start(f32[1536]{0:T(1024)} %param.18) | copy-start | bytes 18436
  446.9 180.7 %copy-start.4 = (f32[3072]{0:T(1024)S(1)}, f32[3072]{0:T(1024)}, u32[]{:S(2)}) copy-start(f32[3072]{0:T(1024)} %param.21) | copy-start | bytes 36868
  499.5 86.9 %all-gather.4.cloned.1.call-start = ((), (), s32[]{:S(2)}) async-start(), calls=%async_computation.3 | async-start | bytes 3538944 | tf_op jit(solution)/shard_map/all_gather | solution.py:80
  546.5 81.1 %reduce-scatter.5.cloned.1.call-start = ((), (), s32[]{:S(2)}) async-start(), calls=%async_computation.5 | async-start | bytes 1966080 | tf_op jit(solution)/shard_map/reduce_scatter | solution.py:97
  597.4 61.7 %reduce-scatter.3.cloned.1.call-start = ((), (), s32[]{:S(2)}) async-start(), calls=%async_computation.4 | async-start | bytes 1474560 | tf_op jit(solution)/shard_map/reduce_scatter | solution.py:94
  603.9 96.9 %all-gather.6.cloned.1.call-start = ((), (), s32[]{:S(2)}) async-start(), calls=%async_computation.6 | async-start | bytes 1966080 | tf_op jit(solution)/shard_map/all_gather | solution.py:108
  707.3 3.5 collective-permute-start
  711.0 36.5 %collective-permute-start.1 = (f32[256,1536]{1,0:T(8,128)S(1)}, f32[256,1536]{1,0:T(8,128)S(1)}, u32[]{:S(2)}, u32[]{:S(2)}) collective-permute-start(f32[256,1536]{1,0:T(8,128)S(1)} %add.89), channel_id=1, source_target_pairs={{0,2},{1,3},{2,0},{3,1},{4,6},{5,7},{6,4},{7,5},{8,10},{9,11},{10,... | collective-permute-start | bytes 4718600 | tf_op jit(solution)/shard_map/ppermute | solution.py:126
  747.7 70.3 %collective-permute-start.2 = (f32[256,1536]{1,0:T(8,128)S(1)}, f32[256,1536]{1,0:T(8,128)S(1)}, u32[]{:S(2)}, u32[]{:S(2)}) collective-permute-start(f32[256,1536]{1,0:T(8,128)S(1)} %add.90), channel_id=1, source_target_pairs={{0,4},{1,5},{2,6},{3,7},{4,0},{5,1},{6,2},{7,3},{8,12},{9,13},{10,... | collective-permute-start | bytes 4718600 | tf_op jit(solution)/shard_map/ppermute | solution.py:126
Sparse Core Ops, SparseCore 0:
  499.6 46.8 all-reduce.1
  548.1 38.1 all-gather.3
  597.5 30.0 reduce-scatter.4
  630.3 28.7 reduce-scatter.2
  660.8 33.7 all-gather.5
